TPU v7x, 32 devices: a whole 2x2x4 slice. The times are simulated.
32 devices in a mesh: row: 4 (over y, x), col: 8 (over z, core).
Axes of the slice: x: 2, y: 2, z: 4, core: 2. Of those that a mesh axis runs over, the one named last changes fastest.
Arguments:
- activations: bfloat16 [256, 16384], P(None, 'row'), may hold values from -3 to 3
- cotangent: bfloat16 [256, 16384], P(None, 'row'), may hold values from -0.59765625 to 0.59765625
- forget: int32 [256], replicated, may hold values 0 or 1
- lengths: int32 [4, 4], P('row'), may hold values from 1 to 32, 64 in all within a row
- query_weight: bfloat16 [16384, 8192], P('row', 'col'), may hold values from -0.046875 to 0.046875
- key_weight: bfloat16 [16384, 512], P('row'), may hold values from -0.046875 to 0.046875
- value_weight: bfloat16 [16384, 512], P('row'), may hold values from -0.046875 to 0.046875
- output_projection_weight: bfloat16 [8192, 16384], P('col', 'row'), may hold values from -0.0625 to 0.0625
- query_down: bfloat16 [16384, 32], P('row'), may hold values from -0.046875 to 0.046875
- query_up: bfloat16 [32, 8192], P(None, 'col'), may hold values from -1 to 1
- output_down: bfloat16 [8192, 32], P('col'), may hold values from -0.0625 to 0.0625
- output_up: bfloat16 [32, 16384], P(None, 'row'), may hold values from -1 to 1
Outputs:
- query_down_gradient: float32 [16384, 32], P('row')
- query_up_gradient: float32 [32, 8192], P(None, 'col')
- output_down_gradient: float32 [8192, 32], P('col')
- output_up_gradient: float32 [32, 16384], P(None, 'row')
Inputs may be any that keep to these rules, and one draw needn't show every extreme that they name: In every row of lengths the 4 values sum to 64, and the largest is exactly 32.
All inputs are finite; a program needn't handle non-finite values.
Results may differ from a plain program's by a relative error of at most 0.025.
Values may be sent and summed in bfloat16 or wider, within the bound.
A program may use at most 128 MiB of HBM per device.

v0:
```python
import math
import jax
import jax.numpy as jnp
from jax import lax
from jax.sharding import PartitionSpec as P

HD = 128
HEADS = 64
KVH = 4
adapter_scale = 0.5
highest_precision = lax.Precision.HIGHEST


def row_contraction(left, right):
    return lax.dot_general(
        left, right, (((1,), (1,)), ((), ())), preferred_element_type=jnp.float32
    )


def token_contraction(left, right):
    return lax.dot_general(
        left, right, (((0,), (0,)), ((), ())), preferred_element_type=jnp.float32
    )


def local(
    activations,
    cotangent,
    forget,
    lengths,
    query_weight,
    key_weight,
    value_weight,
    output_projection_weight,
    query_down,
    query_up,
    output_down,
    output_up,
):
    row_index = lax.axis_index("row")
    col_index = lax.axis_index("col")
    tok_blk = activations.shape[0] // lax.axis_size("row")
    query_cols = query_weight.shape[1]
    heads_dev = query_cols // HD
    group_index = col_index * heads_dev // (HEADS // KVH)
    inverse = 1.0 / math.sqrt(HD)
    up_projection_broad = query_up.astype(jnp.float32)
    down_projection_broad = output_down.astype(jnp.float32)
    key_slice = lax.dynamic_slice_in_dim(key_weight, group_index * HD, HD, 1)
    value_slice = lax.dynamic_slice_in_dim(value_weight, group_index * HD, HD, 1)
    kv_cols = key_slice.shape[1]
    block_of_rows = activations
    reduced_result = jnp.dot(block_of_rows, query_down, preferred_element_type=jnp.float32)
    query_partial_term = jnp.dot(block_of_rows, query_weight, preferred_element_type=jnp.float32)
    query_partial_term = query_partial_term + adapter_scale * jnp.dot(
        reduced_result, up_projection_broad, precision=highest_precision
    )
    key_term = jnp.dot(block_of_rows, key_slice, preferred_element_type=jnp.float32)
    value_term = jnp.dot(block_of_rows, value_slice, preferred_element_type=jnp.float32)
    summed = lax.psum_scatter(
        jnp.concatenate([query_partial_term, key_term, value_term, reduced_result], axis=1).astype(
            jnp.bfloat16
        ),
        "row",
        scatter_dimension=0,
        tiled=True,
    ).astype(jnp.float32)
    query_heads = summed[:, :query_cols].astype(jnp.bfloat16).reshape(tok_blk, heads_dev, HD)
    key_part = summed[:, query_cols : query_cols + kv_cols].astype(jnp.bfloat16)
    value_part = summed[:, query_cols + kv_cols : query_cols + 2 * kv_cols].astype(jnp.bfloat16)
    input_lowrank_factor = summed[:, query_cols + 2 * kv_cols :]
    seg_ends = jnp.cumsum(lengths[0])
    position = jnp.arange(tok_blk, dtype=jnp.int32)
    segment = jnp.sum((position[:, None] >= seg_ends[None, :]).astype(jnp.int32), axis=1)
    allowed = (segment[:, None] == segment[None, :]) & (position[None, :] <= position[:, None])
    scores = (
        jnp.einsum("qhd,kd->hqk", query_heads, key_part, preferred_element_type=jnp.float32)
        * inverse
    )
    numerator = jnp.where(allowed[None], jnp.exp(scores), 0.0)
    softmax = numerator / jnp.sum(numerator, axis=2, keepdims=True)
    weights = softmax.astype(jnp.bfloat16)
    hidden_state = jnp.einsum(
        "hqk,kd->qhd", weights, value_part, preferred_element_type=jnp.float32
    )
    hidden_state = hidden_state.reshape(tok_blk, query_cols).astype(jnp.bfloat16)
    sign_flip = (1 - 2 * forget).astype(jnp.bfloat16)
    output_gradient = cotangent * sign_flip[:, None]
    block_of_rows = output_gradient
    reduced_result = row_contraction(block_of_rows, output_up)
    hidden_state_term = row_contraction(
        block_of_rows, output_projection_weight
    ) + adapter_scale * jnp.dot(
        reduced_result, down_projection_broad.T, precision=highest_precision
    )
    backward = lax.psum_scatter(
        jnp.concatenate([hidden_state_term, reduced_result], axis=1).astype(jnp.bfloat16),
        "row",
        scatter_dimension=0,
        tiled=True,
    ).astype(jnp.float32)
    hidden_grad = backward[:, :query_cols].astype(jnp.bfloat16).reshape(tok_blk, heads_dev, HD)
    gradient_lowrank_factor = backward[:, query_cols:]
    prob_grad = jnp.einsum(
        "qhd,kd->hqk", hidden_grad, value_part, preferred_element_type=jnp.float32
    )
    score_grad = softmax * (prob_grad - jnp.sum(prob_grad * softmax, axis=2, keepdims=True))
    query_gradient = (
        jnp.einsum(
            "hqk,kd->qhd", score_grad, key_part.astype(jnp.float32), precision=highest_precision
        )
        * inverse
    )
    query_gradient = query_gradient.reshape(tok_blk, query_cols)
    query_lowrank_factor = jnp.dot(
        query_gradient, up_projection_broad.T, precision=highest_precision
    )
    hidden_state_factor = jnp.dot(hidden_state, output_down, preferred_element_type=jnp.float32)
    up_projection_piece = adapter_scale * jnp.dot(
        input_lowrank_factor.T, query_gradient, precision=highest_precision
    )
    down_projection_piece = adapter_scale * jnp.dot(
        hidden_state.astype(jnp.float32).T, gradient_lowrank_factor, precision=highest_precision
    )
    query_up_gradient, output_down_gradient = (
        lax.psum(up_projection_piece.astype(jnp.bfloat16), "row").astype(jnp.float32),
        lax.psum(down_projection_piece.astype(jnp.bfloat16), "row").astype(jnp.float32),
    )
    zero_rows = jnp.zeros((activations.shape[0], query_lowrank_factor.shape[1]), jnp.float32)
    first_token = row_index * tok_blk
    query_padded = lax.dynamic_update_slice_in_dim(zero_rows, query_lowrank_factor, first_token, 0)
    hidden_padded = lax.dynamic_update_slice_in_dim(zero_rows, hidden_state_factor, first_token, 0)
    query_total, hidden_total = lax.psum((query_padded, hidden_padded), ("row", "col"))
    query_everywhere = query_total.astype(jnp.bfloat16)
    hidden_state_everywhere = hidden_total.astype(jnp.bfloat16)
    query_down_gradient = adapter_scale * token_contraction(activations, query_everywhere)
    output_up_gradient = adapter_scale * token_contraction(hidden_state_everywhere, output_gradient)
    return (query_down_gradient, query_up_gradient, output_down_gradient, output_up_gradient)


def solution(mesh):
    placed = (
        P(None, "row"),
        P(None, "row"),
        P(),
        P("row", None),
        P("row", "col"),
        P("row", None),
        P("row", None),
        P("col", "row"),
        P("row", None),
        P(None, "col"),
        P("col", None),
        P(None, "row"),
    )
    return jax.shard_map(
        local,
        mesh=mesh,
        in_specs=placed,
        out_specs=(P("row", None), P(None, "col"), P("col", None), P(None, "row")),
        check_vma=False,
    )
```

profile of v0, /device:TPU:0, one launch (start us, length us, event | category | flops | bytes accessed | tf_op | source)
XLA Modules:
  0.0 180.6 jit_solution(12886477900674417634)
XLA Ops:
  7.2 0.0 copy-start
  7.2 0.0 reduce-scatter.3.cloned.1.call-start
  7.2 1.5 copy-done
  8.8 1.7 fusion.58
  10.5 0.1 copy.46
  10.6 1.9 %fusion.17 = bf16[256,128]{1,0:T(8,128)(2,1)S(1)} fusion(bf16[256,4096]{1,0:T(8,128)(2,1)S(1)} %copy-done, bf16[4096,512]{1,0:T(8,128)(2,1)} %param.17, s32[]{:T(128)S(6)} %select_n.18), kind=kOutput, calls=%fused_computation.29 | convolution fusion | flops 268468224 | bytes 3211268 | tf_op jit(solution)/shard_map/dot_general | solution.py:58
  12.5 1.9 %fusion.18 = bf16[256,128]{1,0:T(8,128)(2,1)S(1)} fusion(bf16[256,4096]{1,0:T(8,128)(2,1)S(1)} %copy-done, bf16[4096,512]{1,0:T(8,128)(2,1)} %param.18, s32[]{:T(128)S(6)} %select_n.18), kind=kOutput, calls=%fused_computation.30 | convolution fusion | flops 268468224 | bytes 3211268 | tf_op jit(solution)/shard_map/dot_general | solution.py:59
  14.4 0.0 copy-start.1
  14.4 5.7 %fusion.60 = f32[256,1024]{1,0:T(8,128)S(1)} fusion(bf16[256,4096]{1,0:T(8,128)(2,1)S(1)} %copy-done, bf16[4096,1024]{1,0:T(8,128)(2,1)} %param.16), kind=kOutput, calls=%fused_computation.79 | convolution fusion | flops 2147483648 | bytes 11534336 | tf_op jit(solution)/shard_map/dot_general | solution.py:54
  20.2 0.0 copy-start.4
  20.2 0.0 copy-start.3
  20.2 0.0 copy-done.1
  20.2 0.7 fusion.8
  20.9 0.9 pad_maximum_fusion
  21.8 0.0 reduce-scatter.3.cloned.1.call-update
  21.8 0.0 reduce-scatter.5.cloned.1.call-start
  21.9 0.0 copy-done.4
  21.9 0.0 copy-done.3
  21.9 2.4 %fusion.59 = (bf16[256,32]{0,1:T(8,128)(2,1)S(1)}, f32[256,32]{0,1:T(8,128)S(1)}) fusion(bf16[32,4096]{1,0:T(8,128)(2,1)S(1)} %copy-done.3, bf16[256,4096]{1,0:T(8,128)(2,1)} %param.13, bf16[256]{0:T(256)(128)(2,1)S(1)} %subtract_convert_fusion), kind=kOutput, calls=%fused_computation.78 | convolution fusion | flops 68165632 | bytes 2408960 | tf_op jit(solution)/shard_map/dot_general | solution.py:15
  24.3 0.1 copy.48
  24.5 0.0 copy-start.2
  24.5 6.4 %fusion.4 = f32[256,1024]{1,0:T(8,128)S(1)} fusion(bf16[1024,4096]{1,0:T(8,128)(2,1)} %param.19, bf16[256,4096]{1,0:T(8,128)(2,1)} %param.13, bf16[256]{0:T(256)(128)(2,1)S(1)} %subtract_convert_fusion), kind=kOutput, calls=%fused_computation.6 | convolution fusion | flops 2148532224 | bytes 11534848 | tf_op jit(solution)/shard_map/dot_general | solution.py:15
  30.9 0.0 copy-start.5
  30.9 0.0 copy-done.2
  30.9 0.6 fusion.9
  31.5 0.9 pad_maximum_fusion.1
  32.4 0.0 reduce-scatter.5.cloned.1.call-update
  32.4 0.0 all-reduce.4.cloned.1.call-start
  32.5 0.0 copy-done.5
  32.5 0.2 reduce-window.8
  32.7 0.1 convert_reduce_fusion
  32.8 0.1 fusion.44
  32.8 17.6 %reduce-scatter.3.cloned.1.call-done = bf16[64,1312]{1,0:T(8,128)(2,1)} async-done(((bf16[256,1312]{1,0:T(8,128)(2,1)}), bf16[64,1312]{1,0:T(8,128)(2,1)}) %reduce-scatter.3.cloned.1.call-update) | async-done | bytes 167952 | tf_op jit(solution)/shard_map/reduce_scatter | solution.py:60
  50.4 1.2 fusion.41
  51.7 0.9 fusion.14
  52.6 0.1 fusion.31
  52.7 25.9 %reduce-scatter.5.cloned.1.call-done = bf16[64,1056]{1,0:T(8,128)(2,1)} async-done(((bf16[256,1056]{1,0:T(8,128)(2,1)}), bf16[64,1056]{1,0:T(8,128)(2,1)}) %reduce-scatter.5.cloned.1.call-update) | async-done | bytes 135184 | tf_op jit(solution)/shard_map/reduce_scatter | solution.py:96
  78.7 1.2 multiply_reduce_fusion
  79.8 1.1 fusion.10
  81.0 0.3 fusion.25
  81.2 0.3 dynamic_update_slice.7
  81.6 0.3 dynamic_update_slice.6
  82.0 39.9 %all-reduce = (bf16[256,32]{0,1:T(8,128)(2,1)S(1)}, bf16[256,32]{0,1:T(8,128)(2,1)S(1)}) all-reduce(f32[256,32]{0,1:T(8,128)S(1)} %dynamic_update_slice.6, f32[256,32]{0,1:T(8,128)S(1)} %dynamic_update_slice.7), channel_id=1, replica_groups=mesh['row'=4,'col'=8] {'row','col'}, use_global_device_ids=true, to_apply=%region_6.7 | all-reduce | flops 16384 | bytes 98304 | tf_op jit(solution)/shard_map/psum | solution.py:133
  121.9 2.9 %convolution_multiply_fusion = f32[32,4096]{1,0:T(8,128)} fusion(bf16[256,4096]{1,0:T(8,128)(2,1)} %param.13, bf16[256]{0:T(256)(128)(2,1)S(1)} %subtract_convert_fusion, bf16[256,32]{0,1:T(8,128)(2,1)S(1)} %get-tuple-element.5), kind=kOutput, calls=%fused_computation | convolution fusion | flops 68288512 | bytes 2638336 | tf_op jit(solution)/shard_map/dot_general | solution.py:21
  124.8 1.6 fusion.16
  126.4 1.6 fusion.15
  128.0 0.0 all-reduce.4.cloned.1.call-update
  128.0 1.3 fusion
  129.2 41.8 %all-reduce.4.cloned.1.call-done = (bf16[32,1024]{1,0:T(8,128)(2,1)}, bf16[1024,32]{0,1:T(8,128)(2,1)}) async-done(((bf16[32,1024]{1,0:T(8,128)(2,1)}, bf16[1024,32]{0,1:T(8,128)(2,1)}), (bf16[32,1024]{1,0:T(8,128)(2,1)}, bf16[1024,32]{0,1:T(8,128)(2,1)})) %all-reduce.4.cloned.1.call-update) | async-done | bytes 131088 | tf_op jit(solution)/shard_map/psum | solution.py:126
  171.0 1.5 convert_element_type.52
  172.5 1.5 convert_element_type.58
  (3 shorter events, 0.0 us)
Async XLA Ops:
  7.2 1.6 copy-start
  7.2 43.3 %reduce-scatter.3.cloned.1.call-start = ((), (), s32[]{:S(2)}) async-start(), calls=%async_computation.2 | async-start | bytes 901120 | tf_op jit(solution)/shard_map/reduce_scatter | solution.py:60
  14.4 5.8 %copy-start.1 = (bf16[32,1024]{1,0:T(8,128)(2,1)S(1)}, bf16[32,1024]{1,0:T(8,128)(2,1)}, u32[]{:S(2)}) copy-start(bf16[32,1024]{1,0:T(8,128)(2,1)} %param.21) | copy-start | bytes 196612
  20.2 1.7 copy-start.4
  20.2 1.7 copy-start.3
  21.8 56.8 %reduce-scatter.5.cloned.1.call-start = ((), (), s32[]{:S(2)}) async-start(), calls=%async_computation.3 | async-start | bytes 737280 | tf_op jit(solution)/shard_map/reduce_scatter | solution.py:96
  24.5 6.4 %copy-start.2 = (bf16[1024,32]{0,1:T(8,128)(2,1)S(1)}, bf16[1024,32]{0,1:T(8,128)(2,1)}, u32[]{:S(2)}) copy-start(bf16[1024,32]{0,1:T(8,128)(2,1)} %param.22) | copy-start | bytes 196612
  30.9 1.6 copy-start.5
  32.4 138.6 %all-reduce.4.cloned.1.call-start = ((), (), s32[]{:S(2)}) async-start(), calls=%async_computation.4 | async-start | bytes 262144 | tf_op jit(solution)/shard_map/psum | solution.py:126
Sparse Core Ops, SparseCore 0:
  22.0 28.4 reduce-scatter.2
  53.6 25.0 reduce-scatter.4
  128.1 42.8 all-reduce.3
where the time goes:
time: 181 us
  waiting for transfers between devices  85.3 us (47%)
  blocking collectives  39.9 us (22%)
  matrix products  33.5 us (19%)
  between operations  14 us (8%)
  other arithmetic  5.14 us (3%)
  local copies, waits for them, and re-layouts  2.51 us (1%)
    psum x1, waiting for transfers between devices, local(): lax.psum(up_projection_piece.astype(jnp.bfloat16), 'row')  41.8 us
    psum x1, blocking collectives, local(): lax.psum((query_padded, hidden_padded), ('row', 'col'))  39.9 us
    reduce_scatter x1, waiting for transfers between devices, local(): lax.psum_scatter(jnp.concatenate([hidden_state_term, reduced_result], axi...  25.9 us
    reduce_scatter x1, waiting for transfers between devices, local(): lax.psum_scatter(jnp.concatenate([query_partial_term, key_term, value_ter...  17.6 us
    dot_general x2, matrix products, row_contraction(): lax.dot_general(left, right, (((1,), (1,)), ((), ())), preferred_element_...  8.79 us
    dot_general x1, matrix products, local(): jnp.dot(block_of_rows, query_weight, preferred_element_type=jnp.float32)  5.74 us
    dot_general x2, matrix products, token_contraction(): lax.dot_general(left, right, (((0,), (0,)), ((), ())), preferred_element_...  4.2 us
  transfers between devices with their start and end apart: 3, of which 3 were waited for; matrix products, arithmetic and copies ran while one was open for 8% of the time, Pallas kernels for 0%

commit v1 on v0

--- a/solution.py
+++ b/solution.py
@@ -123,7 +123,9 @@
         hidden_state.astype(jnp.float32).T, gradient_lowrank_factor, precision=highest_precision
     )
     query_up_gradient, output_down_gradient = (
-        lax.psum(up_projection_piece.astype(jnp.bfloat16), "row").astype(jnp.float32),
+        lax.all_gather(up_projection_piece.astype(jnp.bfloat16), "row")
+        .sum(axis=0)
+        .astype(jnp.float32),
         lax.psum(down_projection_piece.astype(jnp.bfloat16), "row").astype(jnp.float32),
     )
     zero_rows = jnp.zeros((activations.shape[0], query_lowrank_factor.shape[1]), jnp.float32)

time: 181 us -> 147 us (0.81)
  waiting for transfers between devices: 85.3 us -> 43.6 us
  blocking collectives: 39.9 us -> 49.9 us
  matrix products: 33.5 us -> 31.3 us
    psum x1, waiting for transfers between devices: 41.8 us -> 0.01 us  [local(): lax.psum(down_projection_piece.astype(jnp.bfloat16), 'row')]
    all_gather x0 -> x1, blocking collectives: none -> 10 us  [local(): lax.all_gather(up_projection_piece.astype(jnp.bfloat16), 'row').sum(axis=0)]
  transfers between devices with their start and end apart: 3 -> 3, of which waited for: 3 -> 2; matrix products, arithmetic and copies ran while one was open for 8% -> 14% of each run, Pallas kernels for 0% -> 0%
where the time goes in v1:
time: 147 us; the launch traced here: 146 us
  blocking collectives  49.9 us (34%)
  waiting for transfers between devices  43.6 us (30%)
  matrix products  31.3 us (21%)
  between operations  14 us (10%)
  other arithmetic  4.35 us (3%)
  local copies, waits for them, and re-layouts  3.02 us (2%)
    psum x1, blocking collectives, local(): lax.psum((query_padded, hidden_padded), ('row', 'col'))  39.9 us
    reduce_scatter x1, waiting for transfers between devices, local(): lax.psum_scatter(jnp.concatenate([hidden_state_term, reduced_result], axi...  25.9 us
    reduce_scatter x1, waiting for transfers between devices, local(): lax.psum_scatter(jnp.concatenate([query_partial_term, key_term, value_ter...  17.6 us
    all_gather x1, blocking collectives, local(): lax.all_gather(up_projection_piece.astype(jnp.bfloat16), 'row').sum(axis=0)  10 us
    dot_general x2, matrix products, row_contraction(): lax.dot_general(left, right, (((1,), (1,)), ((), ())), preferred_element_...  8.79 us
    dot_general x1, matrix products, local(): jnp.dot(block_of_rows, query_weight, preferred_element_type=jnp.float32)  5.74 us
  transfers between devices with their start and end apart: 3, of which 2 were waited for; matrix products, arithmetic and copies ran while one was open for 14% of the time, Pallas kernels for 0%

profile of v1, /device:TPU:0, one launch (start us, length us, event | category | flops | bytes accessed | tf_op | source)
XLA Modules:
  0.0 146.3 jit_solution(2194071299659625554)
XLA Ops:
  7.2 0.0 copy-start
  7.2 0.0 reduce-scatter.3.cloned.1.call-start
  7.2 1.5 %copy-done = bf16[256,4096]{1,0:T(8,128)(2,1)S(1)} copy-done((bf16[256,4096]{1,0:T(8,128)(2,1)S(1)}, bf16[256,4096]{1,0:T(8,128)(2,1)}, u32[]{:S(2)}) %copy-start) | copy-done | bytes 2097176
  8.8 1.7 %fusion.58 = (bf16[256,32]{0,1:T(8,128)(2,1)S(1)}, f32[256,32]{0,1:T(8,128)S(1)}) fusion(bf16[256,4096]{1,0:T(8,128)(2,1)S(1)} %copy-done, bf16[4096,32]{0,1:T(8,128)(2,1)} %param.20), kind=kOutput, calls=%fused_computation.77 | convolution fusion | flops 67117056 | bytes 2408448 | tf_op jit(solution)/shard_map/dot_general | solution.py:53
  10.5 0.1 copy.46
  10.6 1.9 %fusion.17 = bf16[256,128]{1,0:T(8,128)(2,1)S(1)} fusion(bf16[256,4096]{1,0:T(8,128)(2,1)S(1)} %copy-done, bf16[4096,512]{1,0:T(8,128)(2,1)} %param.17, s32[]{:T(128)S(6)} %select_n.18), kind=kOutput, calls=%fused_computation.29 | convolution fusion | flops 268468224 | bytes 3211268 | tf_op jit(solution)/shard_map/dot_general | solution.py:58
  12.5 1.9 %fusion.18 = bf16[256,128]{1,0:T(8,128)(2,1)S(1)} fusion(bf16[256,4096]{1,0:T(8,128)(2,1)S(1)} %copy-done, bf16[4096,512]{1,0:T(8,128)(2,1)} %param.18, s32[]{:T(128)S(6)} %select_n.18), kind=kOutput, calls=%fused_computation.30 | convolution fusion | flops 268468224 | bytes 3211268 | tf_op jit(solution)/shard_map/dot_general | solution.py:59
  14.4 0.0 copy-start.2
  14.4 5.7 %fusion.60 = f32[256,1024]{1,0:T(8,128)S(1)} fusion(bf16[256,4096]{1,0:T(8,128)(2,1)S(1)} %copy-done, bf16[4096,1024]{1,0:T(8,128)(2,1)} %param.16), kind=kOutput, calls=%fused_computation.79 | convolution fusion | flops 2147483648 | bytes 11534336 | tf_op jit(solution)/shard_map/dot_general | solution.py:54
  20.2 0.0 copy-start.5
  20.2 0.0 copy-start.4
  20.2 0.0 copy-done.2
  20.2 0.7 fusion.8
  20.9 0.9 pad_maximum_fusion
  21.8 0.0 reduce-scatter.3.cloned.1.call-update
  21.8 0.0 reduce-scatter.5.cloned.1.call-start
  21.9 0.0 copy-done.5
  21.9 0.0 copy-done.4
  21.9 2.4 %fusion.59 = (bf16[256,32]{0,1:T(8,128)(2,1)S(1)}, f32[256,32]{0,1:T(8,128)S(1)}) fusion(bf16[32,4096]{1,0:T(8,128)(2,1)S(1)} %copy-done.4, bf16[256,4096]{1,0:T(8,128)(2,1)} %param.13, bf16[256]{0:T(256)(128)(2,1)S(1)} %subtract_convert_fusion), kind=kOutput, calls=%fused_computation.78 | convolution fusion | flops 68165632 | bytes 2408960 | tf_op jit(solution)/shard_map/dot_general | solution.py:15
  24.3 0.1 copy.48
  24.5 0.0 copy-start.3
  24.5 6.4 %fusion.4 = f32[256,1024]{1,0:T(8,128)S(1)} fusion(bf16[1024,4096]{1,0:T(8,128)(2,1)} %param.19, bf16[256,4096]{1,0:T(8,128)(2,1)} %param.13, bf16[256]{0:T(256)(128)(2,1)S(1)} %subtract_convert_fusion), kind=kOutput, calls=%fused_computation.6 | convolution fusion | flops 2148532224 | bytes 11534848 | tf_op jit(solution)/shard_map/dot_general | solution.py:15
  30.9 0.0 copy-start.6
  30.9 0.0 copy-done.3
  30.9 0.6 fusion.9
  31.5 0.9 pad_maximum_fusion.1
  32.4 0.0 reduce-scatter.5.cloned.1.call-update
  32.4 0.0 all-reduce.3.cloned.1.call-start
  32.5 0.0 copy-done.6
  32.5 0.2 reduce-window.8
  32.7 0.1 convert_reduce_fusion
  32.8 0.1 fusion.44
  32.8 17.6 %reduce-scatter.3.cloned.1.call-done = bf16[64,1312]{1,0:T(8,128)(2,1)} async-done(((bf16[256,1312]{1,0:T(8,128)(2,1)}), bf16[64,1312]{1,0:T(8,128)(2,1)}) %reduce-scatter.3.cloned.1.call-update) | async-done | bytes 167952 | tf_op jit(solution)/shard_map/reduce_scatter | solution.py:60
  50.4 1.2 fusion.41
  51.7 0.9 fusion.14
  52.6 0.1 fusion.31
  52.7 25.9 %reduce-scatter.5.cloned.1.call-done = bf16[64,1056]{1,0:T(8,128)(2,1)} async-done(((bf16[256,1056]{1,0:T(8,128)(2,1)}), bf16[64,1056]{1,0:T(8,128)(2,1)}) %reduce-scatter.5.cloned.1.call-update) | async-done | bytes 135184 | tf_op jit(solution)/shard_map/reduce_scatter | solution.py:96
  78.7 1.6 %fusion.16 = bf16[1024,32]{0,1:T(8,128)(2,1)} fusion(bf16[8,8,8,128]{3,2,1,0:T(8,128)(2,1)S(1)} %fusion.14, bf16[64,1056]{1,0:T(8,128)(2,1)} %reduce-scatter.5.cloned.1.call-done), kind=kOutput, calls=%fused_computation.28 | convolution fusion | flops 4259840 | bytes 212992 | tf_op jit(solution)/shard_map/dot_general | solution.py:122
  80.2 0.0 all-reduce.3.cloned.1.call-update
  80.2 1.2 multiply_reduce_fusion
  81.4 1.1 fusion.10
  82.5 0.3 fusion.25
  82.8 0.3 dynamic_update_slice.7
  83.2 0.3 dynamic_update_slice.6
  83.5 39.9 %all-reduce = (bf16[256,32]{0,1:T(8,128)(2,1)S(1)}, bf16[256,32]{0,1:T(8,128)(2,1)S(1)}) all-reduce(f32[256,32]{0,1:T(8,128)S(1)} %dynamic_update_slice.6, f32[256,32]{0,1:T(8,128)S(1)} %dynamic_update_slice.7), channel_id=1, replica_groups=mesh['row'=4,'col'=8] {'row','col'}, use_global_device_ids=true, to_apply=%region_6.7 | all-reduce | flops 16384 | bytes 98304 | tf_op jit(solution)/shard_map/psum | solution.py:135
  123.4 0.0 copy-start.1
  123.5 1.3 fusion
  124.7 0.5 copy-done.1
  125.2 1.3 convolution_multiply_fusion
  126.6 1.0 fusion.15
  127.5 10.0 %all-gather = bf16[128,1024]{1,0:T(8,128)(2,1)S(1)} all-gather(bf16[32,1024]{1,0:T(8,128)(2,1)S(1)} %fusion.15), channel_id=2, replica_groups=mesh['row'=4,'col'=8] {'row'}, dimensions={0}, use_global_device_ids=true | all-gather | bytes 327680 | tf_op jit(solution)/shard_map/all_gather | solution.py:126
  137.6 0.7 convert_element_type.54
  138.3 0.0 all-reduce.3.cloned.1.call-done
  138.3 1.5 %convert_element_type.60 = f32[1024,32]{0,1:T(8,128)} convert(bf16[1024,32]{0,1:T(8,128)(2,1)} %all-reduce.3.cloned.1.call-done) | non-fusion elementwise | flops 32768 | bytes 196608 | tf_op jit(solution)/shard_map/convert_element_type | solution.py:129
  (4 shorter events, 0.1 us)
Async XLA Ops:
  7.2 1.6 %copy-start = (bf16[256,4096]{1,0:T(8,128)(2,1)S(1)}, bf16[256,4096]{1,0:T(8,128)(2,1)}, u32[]{:S(2)}) copy-start(bf16[256,4096]{1,0:T(8,128)(2,1)} %param.12) | copy-start | bytes 6291460
  7.2 43.3 %reduce-scatter.3.cloned.1.call-start = ((), (), s32[]{:S(2)}) async-start(), calls=%async_computation.2 | async-start | bytes 901120 | tf_op jit(solution)/shard_map/reduce_scatter | solution.py:60
  14.4 5.8 %copy-start.2 = (bf16[32,1024]{1,0:T(8,128)(2,1)S(1)}, bf16[32,1024]{1,0:T(8,128)(2,1)}, u32[]{:S(2)}) copy-start(bf16[32,1024]{1,0:T(8,128)(2,1)} %param.21) | copy-start | bytes 196612
  20.2 1.7 %copy-start.5 = (s32[256]{0:T(256)S(1)}, s32[256]{0:T(256)}, u32[]{:S(2)}) copy-start(s32[256]{0:T(256)} %param.14) | copy-start | bytes 3076
  20.2 1.7 %copy-start.4 = (bf16[32,4096]{1,0:T(8,128)(2,1)S(1)}, bf16[32,4096]{1,0:T(8,128)(2,1)}, u32[]{:S(2)}) copy-start(bf16[32,4096]{1,0:T(8,128)(2,1)} %param.23) | copy-start | bytes 786436
  21.8 56.8 %reduce-scatter.5.cloned.1.call-start = ((), (), s32[]{:S(2)}) async-start(), calls=%async_computation.3 | async-start | bytes 737280 | tf_op jit(solution)/shard_map/reduce_scatter | solution.py:96
  24.5 6.4 %copy-start.3 = (bf16[1024,32]{0,1:T(8,128)(2,1)S(1)}, bf16[1024,32]{0,1:T(8,128)(2,1)}, u32[]{:S(2)}) copy-start(bf16[1024,32]{0,1:T(8,128)(2,1)} %param.22) | copy-start | bytes 196612
  30.9 1.6 %copy-start.6 = (s32[1,4]{1,0:T(1,128)S(1)}, s32[1,4]{1,0:T(1,128)}, u32[]{:S(2)}) copy-start(s32[1,4]{1,0:T(1,128)} %param.15) | copy-start | bytes 52
  32.4 105.8 %all-reduce.3.cloned.1.call-start = ((), (), s32[]{:S(2)}) async-start(), calls=%async_computation.4 | async-start | bytes 131072 | tf_op jit(solution)/shard_map/psum | solution.py:129
  123.4 1.8 %copy-start.1 = (bf16[256,4096]{1,0:T(8,128)(2,1)S(1)}, bf16[256,4096]{1,0:T(8,128)(2,1)}, u32[]{:S(2)}) copy-start(bf16[256,4096]{1,0:T(8,128)(2,1)} %param.13) | copy-start | bytes 6291460
Sparse Core Ops, SparseCore 0:
  22.0 28.4 reduce-scatter.2
  53.6 25.0 reduce-scatter.4
  82.1 41.4 all-reduce.2
